TPU v7x, 32 devices: a whole 2x2x4 slice. The times are simulated.
32 devices in a mesh: ia: 16 (over z, x, core), jb: 2 (over y).
Axes of the slice: x: 2, y: 2, z: 4, core: 2. Of those that a mesh axis runs over, the one named last changes fastest.
Arguments:
- density: bfloat16 [8000, 100000], P('ia', 'jb'), may hold values from -6 to 6
- chol_vectors: bfloat16 [100000, 32], P('jb', 'ia'), may hold values from -0.01953125 to 0.01953125
- virt_coef: bfloat16 [1000, 1100], P('jb'), may hold values from -0.1875 to 0.1875
Outputs:
- half_back: float32 [8, 32, 1100], P(None, ('ia', 'jb'))
All inputs are finite; a program needn't handle non-finite values.
Results may differ from a plain program's by a relative error of at most 0.0003.
Values may be sent and summed in bfloat16 or wider, within the bound.
A program may use at most 128 MiB of HBM per device.

v0:
```python
import jax
import jax.numpy as jnp
from jax import lax
from jax.sharding import PartitionSpec as P


def from_root(value, axis, source):
    kept = jnp.where(lax.axis_index(axis) == source, value, 0).astype(value.dtype)
    return lax.psum(kept, axis)


def on_device(density, chol_vectors, virt_coef):
    row_count = density.shape[0]
    groups = lax.axis_size("jb")
    slab_devices = lax.axis_size("ia")
    all_vectors = lax.all_gather(chol_vectors, "ia", axis=1, tiled=True)
    gamma_part = jnp.dot(density, all_vectors, preferred_element_type=jnp.float32)
    owner_row = lax.axis_index("ia") % groups
    coef_block = from_root(virt_coef, "jb", owner_row).astype(jnp.float32)
    chol_count = gamma_part.shape[1]
    group_width = chol_count // slab_devices
    reduced = lax.psum_scatter(
        gamma_part.reshape(row_count, slab_devices, group_width),
        "jb",
        scatter_dimension=2,
        tiled=True,
    )
    summed = jnp.einsum("arq,an->rqn", reduced, coef_block, precision=lax.Precision.HIGHEST)
    regrouped = lax.all_to_all(summed, "ia", split_axis=0, concat_axis=0, tiled=True)
    occ_slab = slab_devices // groups
    return jnp.sum(
        regrouped.reshape(occ_slab, groups, regrouped.shape[1], regrouped.shape[2]), axis=1
    )


def solution(mesh):
    in_specs = (P("ia", "jb"), P("jb", "ia"), P("jb", None))
    out_specs = P(None, ("ia", "jb"), None)
    return jax.shard_map(
        on_device, mesh=mesh, in_specs=in_specs, out_specs=out_specs, check_vma=False
    )
```

profile of v0, /device:TPU:0, one launch (start us, length us, event | category | flops | bytes accessed | tf_op | source)
XLA Modules:
  0.0 116.3 jit_solution(9403042419399363401)
XLA Ops:
  7.4 0.0 all-gather.3.cloned.1.call-start
  7.4 0.7 all-gather.3.cloned.1.call-update
  8.1 0.0 all-reduce.2.cloned.1.call-start
  8.2 2.4 %broadcast_select_fusion = bf16[500,1100]{0,1:T(8,128)(2,1)} fusion(bf16[500,1100]{0,1:T(8,128)(2,1)} %param.5, pred[]{:T(512)S(6)} %eq.5), kind=kLoop, calls=%fused_computation.1 | loop fusion | flops 550000 | bytes 2200001 | tf_op jit(solution)/shard_map/jit(_where)/select_n | solution.py:8
  10.5 0.0 all-reduce.2.cloned.1.call-update
  10.6 0.0 reduce-scatter.2.cloned.1.call-start
  10.6 48.0 %all-gather.3.cloned.1.call-done = bf16[16,2,50000]{2,1,0:T(2,128)(2,1)} async-done(((bf16[1,2,50000]{2,1,0:T(2,128)(2,1)}), bf16[16,2,50000]{2,1,0:T(2,128)(2,1)}) %all-gather.3.cloned.1.call-update) | async-done | bytes 3200016 | tf_op jit(solution)/shard_map/all_gather | solution.py:16
  58.6 4.0 %reshape.15 = bf16[32,50000]{1,0:T(8,128)(2,1)S(1)} reshape(bf16[16,2,50000]{2,1,0:T(2,128)(2,1)} %all-gather.3.cloned.1.call-done) | data formatting | bytes 6400000
  62.7 21.3 %fusion.1 = f32[500,32]{0,1:T(8,128)S(1)} fusion(bf16[500,50000]{1,0:T(8,128)(2,1)} %param.3, bf16[32,50000]{1,0:T(8,128)(2,1)S(1)} %reshape.15), kind=kOutput, calls=%fused_computation.3 | convolution fusion | flops 1600000000 | bytes 53264000 | tf_op jit(solution)/shard_map/dot_general | solution.py:17
  84.0 0.6 copy.4
  84.7 0.0 reduce-scatter.2.cloned.1.call-update
  84.7 0.0 all-reduce.2.cloned.1.call-done
  84.7 8.4 %reduce-scatter.2.cloned.1.call-done = f32[500,16,1]{0,1,2:T(8,128)} async-done(((f32[500,16,2]{0,1,2:T(8,128)}), f32[500,16,1]{0,1,2:T(8,128)}) %reduce-scatter.2.cloned.1.call-update) | async-done | bytes 32016 | tf_op jit(solution)/shard_map/reduce_scatter | solution.py:22
  93.1 2.2 %convolution_bitcast_fusion = f32[16,1,1100]{2,0,1:T(8,128)S(1)} fusion(bf16[500,1100]{0,1:T(8,128)(2,1)} %all-reduce.2.cloned.1.call-done, f32[500,16,1]{0,1,2:T(8,128)} %reduce-scatter.2.cloned.1.call-done), kind=kOutput, calls=%fused_computation | convolution fusion | flops 105600000 | bytes 1202400 | tf_op jit(solution)/shard_map/arq,an->rqn/dot_general | solution.py:28
  95.4 0.1 copy.5
  95.5 12.4 %all_to_all.5 = f32[16,1,1100]{2,1,0:T(1,128)S(1)} all-to-all(f32[16,1,1100]{2,1,0:T(1,128)S(1)} %copy.5), channel_id=1, replica_groups=mesh['ia'=16,'jb'=2] {'ia'}, dimensions={0} | all-to-all | bytes 140800 | tf_op jit(solution)/shard_map/all_to_all | solution.py:29
  107.9 0.2 reduce.1
  108.1 0.1 reduce_sum.11
  108.2 0.6 reduce_sum.12
  (2 shorter events, 0.1 us)
Async XLA Ops:
  7.4 51.3 %all-gather.3.cloned.1.call-start = ((), (), s32[]{:S(2)}) async-start(), calls=%async_computation.4 | async-start | bytes 3403264 | tf_op jit(solution)/shard_map/all_gather | solution.py:16
  8.1 76.6 %all-reduce.2.cloned.1.call-start = ((), (), s32[]{:S(2)}) async-start(), calls=%async_computation.3 | async-start | bytes 2260992 | tf_op jit(solution)/shard_map/psum | solution.py:9
  10.6 82.6 %reduce-scatter.2.cloned.1.call-start = ((), (), s32[]{:S(2)}) async-start(), calls=%async_computation.2 | async-start | bytes 98304 | tf_op jit(solution)/shard_map/reduce_scatter | solution.py:22
Sparse Core Ops, SparseCore 0:
  10.3 48.2 all-gather.2
Sparse Core Ops, SparseCore 1:
  10.9 44.4 all-reduce.1
  84.8 8.3 reduce-scatter.1
where the time goes:
time: 117 us; the launch traced here: 116 us
  waiting for transfers between devices  57.2 us (49%)
  matrix products  23.5 us (20%)
  between operations  14.9 us (13%)
  blocking collectives  12.4 us (11%)
  local copies, waits for them, and re-layouts  5.49 us (5%)
  other arithmetic  2.65 us (2%)
    all_gather x1, waiting for transfers between devices, on_device(): all_vectors = lax.all_gather(chol_vectors, 'ia', axis=1, tiled=True)  48 us
    dot_general x1, matrix products, on_device(): jnp.dot(density, all_vectors, preferred_element_type=jnp.float32)  21.3 us
    all_to_all x1, blocking collectives, on_device(): lax.all_to_all(summed, 'ia', split_axis=0, concat_axis=0, tiled=True)  12.4 us
    reduce_scatter x1, waiting for transfers between devices, on_device(): lax.psum_scatter(gamma_part.reshape(row_count, slab_devices, group_width)...  8.41 us
    unnamed x1, local copies, waits for them, and re-layouts  4.04 us
    select_n x1, other arithmetic, from_root(): jnp.where(lax.axis_index(axis) == source, value, 0).astype(value.dtype)  2.38 us
  transfers between devices with their start and end apart: 3, of which 2 were waited for; matrix products, arithmetic and copies ran while one was open for 24% of the time, Pallas kernels for 0%

commit v1 on v0

--- a/solution.py
+++ b/solution.py
@@ -1,7 +1,18 @@
+import functools
+
 import jax
 import jax.numpy as jnp
 from jax import lax
+from jax.experimental import pallas as pl
+from jax.experimental.pallas import tpu as pltpu
 from jax.sharding import PartitionSpec as P
+
+MESH = pl.DeviceIdType.MESH
+LANES = 128
+VMEM_BYTES = 67043328
+MOST_CHUNKS = 15
+AHEAD = 6
+NT = (((1,), (1,)), ((), ()))
 
 
 def from_root(value, axis, source):
@@ -9,7 +20,7 @@
     return lax.psum(kept, axis)
 
 
-def on_device(density, chol_vectors, virt_coef):
+def by_collectives(density, chol_vectors, virt_coef):
     row_count = density.shape[0]
     groups = lax.axis_size("jb")
     slab_devices = lax.axis_size("ia")
@@ -33,9 +44,238 @@
     )
 
 
+def chunks_of(columns):
+    tiles = columns // LANES
+    count = max((c for c in range(1, MOST_CHUNKS + 1) if tiles % c == 0), default=1)
+    return count, tiles // count * LANES, columns - tiles * LANES
+
+
+def kernel(
+    slab, groups, d_hbm, v_hbm, c_hbm, o_ref,
+    dbuf, vbuf, cbuf, acc, gsend, grecv,
+    dsem, tsem, lsem, zs, zr, xs, xr, ks, kr, cs, cr, gs, gr,
+):
+    width, columns = v_hbm.shape
+    count, chunk, tail = chunks_of(columns)
+    last = count - 1
+    line = slab // 4
+    total = slab * groups
+    occ = slab // groups
+    r, g = lax.axis_index("ia"), lax.axis_index("jb")
+    z, x, k = r // 4, (r // 2) % 2, r % 2
+    linear = r * groups + g
+
+    def device(lin):
+        return (lin // groups, lin % groups)
+
+    def place(rr):
+        return ((rr % 2) * 2 + (rr // 2) % 2) * line + rr // 4
+
+    def cols(j):
+        if isinstance(j, int) and j == last:
+            return pl.ds(last * chunk, chunk + tail)
+        return pl.ds(pl.multiple_of(j * chunk, LANES), chunk)
+
+    def rows(start, size):
+        return pl.ds(pl.multiple_of(start * width, width), size * width)
+
+    def d_copy(j):
+        part = pl.ds(pl.multiple_of(j * chunk, LANES), chunk)
+        return pltpu.make_async_copy(d_hbm.at[:, part], dbuf.at[:, part], dsem.at[j])
+
+    rest = pl.ds(count * chunk, tail)
+    d_tail = pltpu.make_async_copy(d_hbm.at[:, rest], dbuf.at[:, rest], tsem) if tail else None
+    own_rows = rows(place(r), 1)
+    v_local = pltpu.make_async_copy(v_hbm, vbuf.at[own_rows, :], lsem.at[0])
+    c_local = pltpu.make_async_copy(c_hbm, cbuf.at[g], lsem.at[1])
+
+    def z_copy(j, step):
+        target = ((z + step) % line * 2 + x) * 2 + k
+        return pltpu.make_async_remote_copy(
+            v_hbm.at[:, cols(j)], vbuf.at[own_rows, cols(j)],
+            zs.at[j, step - 1], zr.at[j, step - 1], device_id=(target, g), device_id_type=MESH,
+        )
+
+    def x_copy(j):
+        part = vbuf.at[rows((k * 2 + x) * line, line), cols(j)]
+        target = (z * 2 + 1 - x) * 2 + k
+        return pltpu.make_async_remote_copy(
+            part, part, xs.at[j], xr.at[j], device_id=(target, g), device_id_type=MESH
+        )
+
+    def k_copy(j):
+        part = vbuf.at[rows(k * 2 * line, 2 * line), cols(j)]
+        target = (z * 2 + x) * 2 + 1 - k
+        return pltpu.make_async_remote_copy(
+            part, part, ks.at[j], kr.at[j], device_id=(target, g), device_id_type=MESH
+        )
+
+    c_copy = pltpu.make_async_remote_copy(
+        c_hbm, cbuf.at[g], cs, cr, device_id=(r, 1 - g), device_id_type=MESH
+    )
+
+    ahead = min(AHEAD, count)
+    for j in range(ahead):
+        d_copy(j).start()
+    if tail:
+        d_tail.start()
+    v_local.start()
+    c_local.start()
+
+    barrier = pltpu.get_barrier_semaphore()
+
+    def greet(step, carry):
+        pl.semaphore_signal(
+            barrier, inc=1, device_id=device((linear + step) % total), device_id_type=MESH
+        )
+        return carry
+
+    lax.fori_loop(1, total, greet, 0)
+    pl.semaphore_wait(barrier, total - 1)
+
+    def z_send(j):
+        for step in range(1, line):
+            z_copy(j, step).start()
+
+    def z_relay(j):
+        for step in range(1, line):
+            z_copy(j, step).wait_recv()
+        x_copy(j).start()
+
+    def x_relay(j):
+        x_copy(j).wait_recv()
+        k_copy(j).start()
+
+    def multiply(j):
+        k_copy(j).wait_recv()
+        d_copy(j).wait()
+        if tail and isinstance(j, int) and j == last:
+            d_tail.wait()
+        acc[...] += lax.dot_general(
+            vbuf[:, cols(j)], dbuf[:, cols(j)], NT, preferred_element_type=jnp.float32
+        )
+
+    def looped(f, start, stop):
+        def body(j, carry):
+            f(j)
+            return carry
+
+        lax.fori_loop(start, stop, body, 0)
+
+    looped(z_send, 0, last)
+    z_send(last)
+    c_copy.start()
+    acc[...] = jnp.zeros_like(acc)
+    v_local.wait()
+    z_relay(0)
+    z_relay(1)
+    x_relay(0)
+
+    def step_of(j):
+        z_relay(j + 2)
+        x_relay(j + 1)
+
+        @pl.when(j + ahead < count)
+        def _():
+            d_copy(j + ahead).start()
+
+        multiply(j)
+
+    looped(step_of, 0, count - 3)
+    z_relay(last)
+    x_relay(last - 1)
+    multiply(count - 3)
+    x_relay(last)
+    multiply(count - 2)
+    multiply(last)
+
+    gsend[:, 0, :] = acc[...]
+
+    def g_copy(step):
+        target = (linear + step) % total
+        tr, tg = device(target)
+        return pltpu.make_async_remote_copy(
+            gsend.at[place(tr) * width + tg], grecv.at[g, r % groups, r // groups],
+            gs.at[step], gr.at[step], device_id=(tr, tg), device_id_type=MESH,
+        )
+
+    looped(lambda step: g_copy(step).start(), 1, total)
+    g_local = pltpu.make_async_copy(
+        gsend.at[place(r) * width + g], grecv.at[g, r % groups, r // groups], lsem.at[2]
+    )
+    g_local.start()
+
+    def sent(j):
+        for step in range(1, line):
+            z_copy(j, step).wait_send()
+        x_copy(j).wait_send()
+        k_copy(j).wait_send()
+
+    looped(sent, 0, last)
+    sent(last)
+    c_local.wait()
+    c_copy.wait()
+    g_local.wait()
+    looped(lambda step: g_copy(step).wait_recv(), 1, total)
+
+    total_out = None
+    for half in range(groups):
+        gam = sum(grecv[src, half, :, 0, :] for src in range(1, groups)) + grecv[0, half, :, 0, :]
+        high = gam.astype(jnp.bfloat16).astype(jnp.float32)
+        left = gam - high
+        mid = left.astype(jnp.bfloat16).astype(jnp.float32)
+        low = left - mid
+        stacked = jnp.concatenate([high, mid, low], axis=0).astype(jnp.bfloat16)
+        part = lax.dot_general(stacked, cbuf[half], NT, preferred_element_type=jnp.float32)
+        total_out = part if total_out is None else total_out + part
+    o_ref[...] = total_out[2 * occ:] + total_out[occ:2 * occ] + total_out[:occ]
+    looped(lambda step: g_copy(step).wait_send(), 1, total)
+
+
+def fused(slab, groups, density, chol_vectors, virt_coef):
+    rows, columns = density.shape
+    width = chol_vectors.shape[1]
+    coef_rows, orbitals = virt_coef.shape
+    count = chunks_of(columns)[0]
+    line, total, occ = slab // 4, slab * groups, slab // groups
+    dma = pltpu.SemaphoreType.DMA
+    out = pl.pallas_call(
+        functools.partial(kernel, slab, groups),
+        out_shape=jax.ShapeDtypeStruct((occ, orbitals), jnp.float32),
+        in_specs=[pl.BlockSpec(memory_space=pl.ANY)] * 3,
+        out_specs=pl.BlockSpec(memory_space=pltpu.VMEM),
+        scratch_shapes=[
+            pltpu.VMEM((rows, columns), density.dtype),
+            pltpu.VMEM((slab * width, columns), chol_vectors.dtype),
+            pltpu.VMEM((groups, orbitals, coef_rows), virt_coef.dtype),
+            pltpu.VMEM((slab * width, rows), jnp.float32),
+            pltpu.VMEM((slab * width, 1, rows), jnp.float32),
+            pltpu.VMEM((groups, groups, occ, 1, rows), jnp.float32),
+            dma((count,)), dma, dma((3,)),
+            dma((count, line - 1)), dma((count, line - 1)),
+            dma((count,)), dma((count,)), dma((count,)), dma((count,)),
+            dma, dma, dma((total,)), dma((total,)),
+        ],
+        compiler_params=pltpu.CompilerParams(
+            collective_id=0, has_side_effects=True, vmem_limit_bytes=VMEM_BYTES
+        ),
+    )(density, chol_vectors.T, virt_coef.T)
+    return out.reshape(occ, 1, orbitals)
+
+
+def on_device(slab, groups, density, chol_vectors, virt_coef):
+    rows, columns = density.shape
+    width = chol_vectors.shape[1]
+    padded = (columns + LANES) * (rows + 16 + slab * width) * 2
+    fits = padded + 8 * virt_coef.size < VMEM_BYTES - (6 << 20)
+    paired = groups == 2 and width == groups and slab % 8 == 0
+    if fits and paired and rows == virt_coef.shape[0] and chunks_of(columns)[0] >= 4:
+        return fused(slab, groups, density, chol_vectors, virt_coef)
+    return by_collectives(density, chol_vectors, virt_coef)
+
+
 def solution(mesh):
     in_specs = (P("ia", "jb"), P("jb", "ia"), P("jb", None))
     out_specs = P(None, ("ia", "jb"), None)
-    return jax.shard_map(
-        on_device, mesh=mesh, in_specs=in_specs, out_specs=out_specs, check_vma=False
-    )
+    body = functools.partial(on_device, mesh.shape["ia"], mesh.shape["jb"])
+    return jax.shard_map(body, mesh=mesh, in_specs=in_specs, out_specs=out_specs, check_vma=False)

time: 117 us -> 54.9 us (0.47)
  waiting for transfers between devices: 57.2 us -> 0 us
  Pallas kernels: 0 us -> 53.3 us
  matrix products: 23.5 us -> 0 us
  between operations: 14.9 us -> 0.01 us
  blocking collectives: 12.4 us -> 0 us
  local copies, waits for them, and re-layouts: 5.49 us -> 1.42 us
  other arithmetic: 2.65 us -> 0 us
    pallas_call x0 -> x1, Pallas kernels: none -> 53.3 us  [fused(): pl.pallas_call(functools.partial(kernel, slab, groups), out_shape=jax.Sha...]
    all_gather x1 -> x0, waiting for transfers between devices: 48 us -> none  [on_device(): all_vectors = lax.all_gather(chol_vectors, 'ia', axis=1, tiled=True)]
    dot_general x2 -> x0, matrix products: 23.5 us -> none  [the longest x1 21.3 us: on_device(): jnp.dot(density, all_vectors, preferred_element_type=jnp.float32)]
    all_to_all x1 -> x0, blocking collectives: 12.4 us -> none  [on_device(): lax.all_to_all(summed, 'ia', split_axis=0, concat_axis=0, tiled=True)]
    reduce_scatter x1 -> x0, waiting for transfers between devices: 8.41 us -> none  [on_device(): lax.psum_scatter(gamma_part.reshape(row_count, slab_devices, group_width)...]
    unnamed x1 -> x0, local copies, waits for them, and re-layouts: 4.04 us -> none
    select_n x1 -> x0, other arithmetic: 2.38 us -> none  [from_root(): jnp.where(lax.axis_index(axis) == source, value, 0).astype(value.dtype)]
  transfers between devices with their start and end apart: 3 -> 0, of which waited for: 2 -> 0; matrix products, arithmetic and copies ran while one was open for 24% -> 0% of each run, Pallas kernels for 0% -> 0%
where the time goes in v1:
time: 54.9 us; the launch traced here: 54.8 us
  Pallas kernels  53.3 us (97%)
  local copies, waits for them, and re-layouts  1.42 us (3%)
    pallas_call x1, Pallas kernels, fused(): pl.pallas_call(functools.partial(kernel, slab, groups), out_shape=jax.Sha...  53.3 us
    reshape x1, local copies, waits for them, and re-layouts, fused(): return out.reshape(occ, 1, orbitals)  1.42 us

profile of v1, /device:TPU:0, one launch (start us, length us, event | category | flops | bytes accessed | tf_op | source)
XLA Modules:
  0.0 54.8 jit_solution(9210947590317036164)
XLA Ops:
  0.0 53.3 %shard_map.37 = f32[8,1100]{1,0:T(8,128)} custom-call(bf16[500,50000]{1,0:T(8,128)(2,1)} %d_hbm.1, bf16[2,50000]{1,0:T(2,128)(2,1)} %bitcast.4, bf16[1100,500]{1,0:T(8,128)(2,1)} %bitcast.3), custom_call_target="tpu_custom_call" | custom-call | tf_op jit(solution)/shard_map/pallas_call | solution.py:242
  53.3 1.4 %copy.4 = f32[8,1,1100]{2,1,0:T(1,128)} copy(f32[8,1,1100]{2,0,1:T(8,128)} %bitcast.5) | data formatting | bytes 70400 | tf_op jit(solution)/shard_map/reshape | solution.py:263

commit v2 on v1

--- a/solution.py
+++ b/solution.py
@@ -12,6 +12,7 @@
 VMEM_BYTES = 67043328
 MOST_CHUNKS = 15
 AHEAD = 6
+LAG = 3
 NT = (((1,), (1,)), ((), ()))
 
 
@@ -110,9 +111,26 @@
             part, part, ks.at[j], kr.at[j], device_id=(target, g), device_id_type=MESH
         )
 
-    c_copy = pltpu.make_async_remote_copy(
-        c_hbm, cbuf.at[g], cs, cr, device_id=(r, 1 - g), device_id_type=MESH
-    )
+    orbitals = c_hbm.shape[0]
+    cut = orbitals // 32 * 16
+    halves = (pl.ds(0, cut), pl.ds(cut, orbitals - cut))
+
+    def c_over(half):
+        return pltpu.make_async_remote_copy(
+            c_hbm.at[halves[half], :], cbuf.at[g, halves[half], :], cs.at[0], cr.at[0],
+            device_id=(r, 1 - g), device_id_type=MESH,
+        )
+
+    def c_across(half):
+        part = cbuf.at[1 - g, halves[half], :]
+        target = (z * 2 + x) * 2 + 1 - k
+        return pltpu.make_async_remote_copy(
+            part, part, cs.at[1], cr.at[1], device_id=(target, g), device_id_type=MESH
+        )
+
+    def by_core(f):
+        for half in range(2):
+            pl.when(k == half)(functools.partial(f, half))
 
     ahead = min(AHEAD, count)
     for j in range(ahead):
@@ -164,30 +182,37 @@
 
     looped(z_send, 0, last)
     z_send(last)
-    c_copy.start()
+    by_core(lambda half: c_over(half).start())
     acc[...] = jnp.zeros_like(acc)
     v_local.wait()
-    z_relay(0)
-    z_relay(1)
-    x_relay(0)
-
-    def step_of(j):
-        z_relay(j + 2)
-        x_relay(j + 1)
-
-        @pl.when(j + ahead < count)
-        def _():
+
+    def step_of(t):
+        fixed = isinstance(t, int)
+        if not fixed or t < count:
+            z_relay(t)
+        if not fixed or 0 <= t - LAG < count:
+            x_relay(t - LAG)
+        j = t - LAG - 1
+        if not fixed:
+            @pl.when(j + ahead < count)
+            def _():
+                d_copy(j + ahead).start()
+        elif 0 <= j and j + ahead < count:
             d_copy(j + ahead).start()
-
-        multiply(j)
-
-    looped(step_of, 0, count - 3)
-    z_relay(last)
-    x_relay(last - 1)
-    multiply(count - 3)
-    x_relay(last)
-    multiply(count - 2)
-    multiply(last)
+        if not fixed or j >= 0:
+            multiply(j)
+
+    def c_pass(half):
+        c_over(half).wait_recv()
+        c_across(half).start()
+
+    for t in range(LAG + 1):
+        step_of(t)
+    looped(step_of, LAG + 1, last)
+    step_of(last)
+    by_core(c_pass)
+    for t in range(count, count + LAG + 1):
+        step_of(t)
 
     gsend[:, 0, :] = acc[...]
 
@@ -214,7 +239,13 @@
     looped(sent, 0, last)
     sent(last)
     c_local.wait()
-    c_copy.wait()
+
+    def c_done(half):
+        c_over(half).wait_send()
+        c_across(half).wait_send()
+        c_across(1 - half).wait_recv()
+
+    by_core(c_done)
     g_local.wait()
     looped(lambda step: g_copy(step).wait_recv(), 1, total)
 
@@ -254,7 +285,7 @@
             dma((count,)), dma, dma((3,)),
             dma((count, line - 1)), dma((count, line - 1)),
             dma((count,)), dma((count,)), dma((count,)), dma((count,)),
-            dma, dma, dma((total,)), dma((total,)),
+            dma((2,)), dma((2,)), dma((total,)), dma((total,)),
         ],
         compiler_params=pltpu.CompilerParams(
             collective_id=0, has_side_effects=True, vmem_limit_bytes=VMEM_BYTES
@@ -269,7 +300,7 @@
     padded = (columns + LANES) * (rows + 16 + slab * width) * 2
     fits = padded + 8 * virt_coef.size < VMEM_BYTES - (6 << 20)
     paired = groups == 2 and width == groups and slab % 8 == 0
-    if fits and paired and rows == virt_coef.shape[0] and chunks_of(columns)[0] >= 4:
+    if fits and paired and rows == virt_coef.shape[0] and chunks_of(columns)[0] > LAG + 2:
         return fused(slab, groups, density, chol_vectors, virt_coef)
     return by_collectives(density, chol_vectors, virt_coef)
 

time: 54.9 us -> 46.8 us (0.85)
  Pallas kernels: 53.3 us -> 45.2 us
    pallas_call x1, Pallas kernels: 53.3 us -> 45.2 us  [fused(): pl.pallas_call(functools.partial(kernel, slab, groups), out_shape=jax.Sha...]
where the time goes in v2:
time: 46.8 us; the launch traced here: 46.6 us
  Pallas kernels  45.2 us (97%)
  local copies, waits for them, and re-layouts  1.42 us (3%)
    pallas_call x1, Pallas kernels, fused(): pl.pallas_call(functools.partial(kernel, slab, groups), out_shape=jax.Sha...  45.2 us
    reshape x1, local copies, waits for them, and re-layouts, fused(): return out.reshape(occ, 1, orbitals)  1.42 us

profile of v2, /device:TPU:0, one launch (start us, length us, event | category | flops | bytes accessed | tf_op | source)
XLA Modules:
  0.0 46.6 jit_solution(6289528020838161649)
XLA Ops:
  0.0 45.2 %shard_map.37 = f32[8,1100]{1,0:T(8,128)} custom-call(bf16[500,50000]{1,0:T(8,128)(2,1)} %d_hbm.1, bf16[2,50000]{1,0:T(2,128)(2,1)} %bitcast.4, bf16[1100,500]{1,0:T(8,128)(2,1)} %bitcast.3), custom_call_target="tpu_custom_call" | custom-call | tf_op jit(solution)/shard_map/pallas_call | solution.py:273
  45.2 1.4 %copy.4 = f32[8,1,1100]{2,1,0:T(1,128)} copy(f32[8,1,1100]{2,0,1:T(8,128)} %bitcast.5) | data formatting | bytes 70400 | tf_op jit(solution)/shard_map/reshape | solution.py:294
